TPU v7x, 128 devices: a whole 4x4x4 slice. The times are simulated.
128 devices in a mesh: grp: 8 (over x_hi, z), mem: 16 (over y, x_lo, core).
Axes of the slice: x: 4 (x_hi: 2, x_lo: 2; x = x_hi * 2 + x_lo), y: 4, z: 4, core: 2. Of those that a mesh axis runs over, the one named last changes fastest.
Arguments:
- candidates: bfloat16 [131072, 4096], P(('grp', 'mem')), may hold values from -1 to 1
- round_one: bfloat16 [8192, 4096], P(('grp', 'mem')), may hold values from -1 to 1
- counts: int32 [8, 16], P('grp', 'mem'), may hold values from 1 to 64, 384 in all within a row
- chosen: int32 [8, 128], P('grp'), may hold values from 0 to 383, as said below
Outputs:
- group_dist: float32 [131072], P(('grp', 'mem'))
- final_dist: float32 [131072], P(('grp', 'mem'))
Inputs may be any that keep to these rules, and one draw needn't show every extreme that they name: In each group the counts sum to 384, and some device of each group has exactly 64. `chosen`: within a group the 128 positions are distinct, each below 384.
All inputs are finite; a program needn't handle non-finite values.
Results may differ from a plain program's by a relative error of at most 0.0003.
Values may be sent and summed in bfloat16 or wider, within the bound.
A program may use at most 128 MiB of HBM per device.

v0:
```python
import jax
import jax.numpy as jnp
from jax import lax
from jax.sharding import PartitionSpec as P


def sq_norms(matrix):
    return jnp.sum(jnp.square(matrix.astype(jnp.float32)), axis=1)


def distances(cand_rows, cand_norm, center_rows):
    inner = lax.dot_general(
        cand_rows, center_rows, (((1,), (1,)), ((), ())), preferred_element_type=jnp.float32
    )
    return cand_norm[:, None] + sq_norms(center_rows)[None, :] - 2.0 * inner


def lookup(table, index_values):
    entries = jnp.arange(table.shape[0], dtype=jnp.int32)
    match = index_values[:, None] == entries[None, :]
    return jnp.sum(jnp.where(match, table[None, :], 0), axis=1)


def body(candidates, round_one, counts, chosen):
    mem_size = lax.axis_size("mem")
    my_index = lax.axis_index("mem")
    slot_max = round_one.shape[0]
    width = round_one.shape[1]
    picks_total = chosen.shape[1]
    group_counts = lax.all_gather(counts, "mem", axis=1, tiled=True)[0]
    offsets = jnp.cumsum(group_counts) - group_counts
    picked_ids = chosen[0]
    cand_norm = sq_norms(candidates)
    start_state = (
        jnp.full((candidates.shape[0],), jnp.inf, jnp.float32),
        jnp.zeros((picks_total, width), jnp.float32),
    )
    block_rows = lax.all_gather(round_one, "mem", axis=0, tiled=True)
    slot_ids = jnp.arange(block_rows.shape[0], dtype=jnp.int32)
    holder = slot_ids // slot_max
    within = slot_ids % slot_max
    usable = within < lookup(group_counts, holder)
    position = lookup(offsets, holder) + within
    gaps = distances(candidates, cand_norm, block_rows)
    gaps = jnp.where(usable[None, :], gaps, jnp.inf)
    nearest = jnp.minimum(start_state[0], jnp.min(gaps, axis=1))
    select = ((picked_ids[:, None] == position[None, :]) & usable[None, :]).astype(jnp.bfloat16)
    collected = jnp.dot(select, block_rows, preferred_element_type=jnp.float32)
    nearest, collected = (nearest, collected)
    picked = collected.astype(jnp.bfloat16)
    final_start = jnp.full((candidates.shape[0],), jnp.inf, jnp.float32)
    share = picks_total // mem_size
    my_share = lax.dynamic_slice_in_dim(picked, my_index * share, share, 0)
    final = jnp.minimum(
        final_start,
        jnp.min(
            distances(
                candidates, cand_norm, lax.all_gather(my_share, ("grp", "mem"), axis=0, tiled=True)
            ),
            axis=1,
        ),
    )
    return (nearest, final)


def solution(mesh):
    in_specs = (P(("grp", "mem"), None), P(("grp", "mem"), None), P("grp", "mem"), P("grp", None))
    out_specs = (P(("grp", "mem")), P(("grp", "mem")))
    return jax.shard_map(body, mesh=mesh, in_specs=in_specs, out_specs=out_specs, check_vma=False)
```

profile of v0, /device:TPU:1, one launch (start us, length us, event | category | flops | bytes accessed | tf_op | source)
XLA Modules:
  0.0 298.8 jit_solution(11337238122814754986)
XLA Ops:
  7.2 0.0 all-gather.3.cloned.1.call-start
  7.2 0.7 all-gather.3.cloned.1.call-update
  7.9 0.0 all-gather.5.cloned.1.call-start
  8.6 1.2 dynamic-slice
  9.8 0.7 bitcast_dynamic-update-slice_fusion
  10.5 11.0 %all-reduce = s32[16]{0:T(128)S(1)} all-reduce(s32[16]{0:T(128)S(1)} %bitcast_dynamic-update-slice_fusion), channel_id=1, replica_groups=mesh['grp'=8,'mem'=16] {'mem'}, use_global_device_ids=true, to_apply=%add | all-reduce | flops 16 | bytes 128
  21.5 0.2 reduce-window_clone.1
  21.7 0.1 select_reduce_fusion.1
  21.8 43.6 %all-gather.3.cloned.1.call-done = bf16[1024,4096]{1,0:T(8,128)(2,1)} async-done(((bf16[64,4096]{1,0:T(8,128)(2,1)}), bf16[1024,4096]{1,0:T(8,128)(2,1)}) %all-gather.3.cloned.1.call-update) | async-done | bytes 8388624 | tf_op jit(solution)/shard_map/all_gather | solution.py:38
  65.5 4.7 %fusion.1 = bf16[128,4096]{1,0:T(8,128)(2,1)S(1)} fusion(bf16[1024,4096]{1,0:T(8,128)(2,1)} %all-gather.3.cloned.1.call-done, s32[1024]{0:T(1024)S(1)} %fusion.10, s32[128]{0:T(128)} %bitcast.17, pred[1024]{0:T(1024)(128)(4,1)S(1)} %fusion.11), kind=kOutput, calls=%fused_computation.6 | convolution fusion | flops 1074003968 | bytes 9442816 | tf_op jit(solution)/shard_map/dot_general | solution.py:48
  70.2 0.6 dynamic-slice_convert_fusion
  70.8 0.0 all-gather.5.cloned.1.call-update
  70.8 0.0 copy-start
  70.8 5.2 %multiply_reduce_fusion.2 = f32[1024]{0:T(1024)S(1)} fusion(bf16[1024,4096]{1,0:T(8,128)(2,1)} %param.4), kind=kLoop, calls=%fused_computation.2 | loop fusion | flops 12581888 | bytes 8392704 | tf_op jit(solution)/shard_map/reduce_sum | solution.py:8
  76.1 0.5 copy-done
  76.6 1.7 multiply_reduce_fusion.1
  78.3 12.3 %select_reduce_fusion = f32[1024]{0:T(1024)} fusion(bf16[1024,4096]{1,0:T(8,128)(2,1)} %param.4, bf16[1024,4096]{1,0:T(8,128)(2,1)S(1)} %copy-done, f32[1024]{0:T(1024)S(1)} %multiply_reduce_fusion.1, f32[1024]{0:T(1024)S(1)} %multiply_reduce_fusion.2, pred[1024]{0:T(1024)(128)(4,1)S(1)} %fusion.11), kind=kOutput, calls=%fused_computation.5 | convolution fusion | flops 8595176448 | bytes 16790528 | tf_op jit(solution)/shard_map/dot_general | solution.py:12
  90.6 183.8 %all-gather.5.cloned.1.call-done = bf16[1024,4096]{1,0:T(8,128)(2,1)} async-done(((bf16[8,4096]{1,0:T(8,128)(2,1)}), bf16[1024,4096]{1,0:T(8,128)(2,1)}) %all-gather.5.cloned.1.call-update) | async-done | bytes 8388624 | tf_op jit(solution)/shard_map/all_gather | solution.py:58
  274.3 0.0 copy-start.1
  274.3 5.2 %multiply_reduce_fusion = f32[1024]{0:T(1024)S(1)} fusion(bf16[1024,4096]{1,0:T(8,128)(2,1)} %all-gather.5.cloned.1.call-done), kind=kLoop, calls=%fused_computation | loop fusion | flops 12581888 | bytes 8392704 | tf_op jit(solution)/shard_map/reduce_sum | solution.py:8
  279.5 0.5 copy-done.1
  280.1 11.9 %fusion = f32[1024]{0:T(1024)} fusion(bf16[1024,4096]{1,0:T(8,128)(2,1)S(1)} %copy-done.1, bf16[1024,4096]{1,0:T(8,128)(2,1)} %param.4, f32[1024]{0:T(1024)S(1)} %multiply_reduce_fusion, f32[1024]{0:T(1024)S(1)} %multiply_reduce_fusion.2), kind=kOutput, calls=%fused_computation.4 | convolution fusion | flops 8594127872 | bytes 16789504 | tf_op jit(solution)/shard_map/dot_general | solution.py:12
  (5 shorter events, 0.0 us)
Async XLA Ops:
  7.2 58.3 %all-gather.3.cloned.1.call-start = ((), (), s32[]{:S(2)}) async-start(), calls=%async_computation | async-start | bytes 8912896 | tf_op jit(solution)/shard_map/all_gather | solution.py:38
  7.9 266.4 %all-gather.5.cloned.1.call-start = ((), (), s32[]{:S(2)}) async-start(), calls=%async_computation.1 | async-start | bytes 8454144 | tf_op jit(solution)/shard_map/all_gather | solution.py:58
  70.8 5.8 %copy-start = (bf16[1024,4096]{1,0:T(8,128)(2,1)S(1)}, bf16[1024,4096]{1,0:T(8,128)(2,1)}, u32[]{:S(2)}) copy-start(bf16[1024,4096]{1,0:T(8,128)(2,1)} %all-gather.3.cloned.1.call-done) | copy-start | bytes 25165828
  274.3 5.8 %copy-start.1 = (bf16[1024,4096]{1,0:T(8,128)(2,1)S(1)}, bf16[1024,4096]{1,0:T(8,128)(2,1)}, u32[]{:S(2)}) copy-start(bf16[1024,4096]{1,0:T(8,128)(2,1)} %all-gather.5.cloned.1.call-done) | copy-start | bytes 25165828
Sparse Core Ops, SparseCore 0:
  9.7 55.7 all-gather.2
  70.9 203.3 all-gather.4
where the time goes:
time: 299 us
  waiting for transfers between devices  228 us (76%)
  matrix products  28.8 us (10%)
  between operations  14.7 us (5%)
  other arithmetic  12.4 us (4%)
  blocking collectives  11 us (4%)
  local copies, waits for them, and re-layouts  3.63 us (1%)
    all_gather x1, waiting for transfers between devices, body(): lax.all_gather(my_share, ('grp', 'mem'), axis=0, tiled=True)  184 us
    all_gather x1, waiting for transfers between devices, body(): block_rows = lax.all_gather(round_one, 'mem', axis=0, tiled=True)  43.6 us
    dot_general x2, matrix products, distances(): lax.dot_general(cand_rows, center_rows, (((1,), (1,)), ((), ())), preferr...  24.1 us
    reduce_sum x3, other arithmetic, sq_norms(): return jnp.sum(jnp.square(matrix.astype(jnp.float32)), axis=1)  12.1 us
    unnamed x1, blocking collectives  11 us
  transfers between devices with their start and end apart: 2, of which 2 were waited for; matrix products, arithmetic and copies ran while one was open for 7% of the time, Pallas kernels for 0%

commit v1 on v0

--- a/solution.py
+++ b/solution.py
@@ -55,7 +55,14 @@
         final_start,
         jnp.min(
             distances(
-                candidates, cand_norm, lax.all_gather(my_share, ("grp", "mem"), axis=0, tiled=True)
+                candidates,
+                cand_norm,
+                jnp.concatenate(
+                    lax.all_to_all(
+                        jnp.stack([my_share] * lax.axis_size(("grp", "mem"))), ("grp", "mem"), 0, 0
+                    ),
+                    axis=0,
+                ),
             ),
             axis=1,
         ),

time: 299 us -> 220 us (0.74)
  the two profiles are of different devices: /device:TPU:1 before, /device:TPU:14 now
where the time goes in v1:
time: 220 us; the launch traced here: 219 us
  waiting for transfers between devices  131 us (60%)
  matrix products  31.4 us (14%)
  other arithmetic  15.8 us (7%)
  between operations  14.8 us (7%)
  blocking collectives  10.5 us (5%)
  starting transfers between devices  9.7 us (4%)
  local copies, waits for them, and re-layouts  6.3 us (3%)
    all_to_all x1, waiting for transfers between devices, body(): lax.all_to_all(jnp.stack([my_share] * lax.axis_size(('grp', 'mem'))), ('g...  87.5 us
    all_gather x1, waiting for transfers between devices, body(): block_rows = lax.all_gather(round_one, 'mem', axis=0, tiled=True)  42.7 us
    dot_general x2, matrix products, distances(): lax.dot_general(cand_rows, center_rows, (((1,), (1,)), ((), ())), preferr...  26.7 us
    reduce_sum x3, other arithmetic, sq_norms(): return jnp.sum(jnp.square(matrix.astype(jnp.float32)), axis=1)  15.5 us
    unnamed x1, blocking collectives  10.5 us
    all_to_all x1, starting transfers between devices, body(): lax.all_to_all(jnp.stack([my_share] * lax.axis_size(('grp', 'mem'))), ('g...  9.66 us
    dot_general x1, matrix products, body(): collected = jnp.dot(select, block_rows, preferred_element_type=jnp.float32)  4.69 us
  transfers between devices with their start and end apart: 2, of which 2 were waited for; matrix products, arithmetic and copies ran while one was open for 11% of the time, Pallas kernels for 0%

profile of v1, /device:TPU:14, one launch (start us, length us, event | category | flops | bytes accessed | tf_op | source)
XLA Modules:
  0.0 219.3 jit_solution(16794981724334185637)
XLA Ops:
  7.2 0.0 all-gather.2.cloned.1.call-start
  7.2 0.7 all-gather.2.cloned.1.call-update
  8.5 1.2 dynamic-slice
  9.8 0.7 bitcast_dynamic-update-slice_fusion
  10.5 10.5 %all-reduce = s32[16]{0:T(128)S(1)} all-reduce(s32[16]{0:T(128)S(1)} %bitcast_dynamic-update-slice_fusion), channel_id=1, replica_groups=mesh['grp'=8,'mem'=16] {'mem'}, use_global_device_ids=true, to_apply=%add | all-reduce | flops 16 | bytes 128
  21.0 0.2 reduce-window_clone.1
  21.2 0.1 select_reduce_fusion.1
  21.3 42.7 %all-gather.2.cloned.1.call-done = bf16[1024,4096]{1,0:T(8,128)(2,1)} async-done(((bf16[64,4096]{1,0:T(8,128)(2,1)}), bf16[1024,4096]{1,0:T(8,128)(2,1)}) %all-gather.2.cloned.1.call-update) | async-done | bytes 8388624 | tf_op jit(solution)/shard_map/all_gather | solution.py:38
  64.0 4.7 %fusion.5 = bf16[128,4096]{1,0:T(8,128)(2,1)S(1)} fusion(bf16[1024,4096]{1,0:T(8,128)(2,1)} %all-gather.2.cloned.1.call-done, s32[1024]{0:T(1024)S(1)} %fusion.14, s32[128]{0:T(128)} %bitcast.23, pred[1024]{0:T(1024)(128)(4,1)S(1)} %fusion.15), kind=kOutput, calls=%fused_computation.8 | convolution fusion | flops 1074003968 | bytes 9442816 | tf_op jit(solution)/shard_map/dot_general | solution.py:48
  68.7 4.3 %stack.2 = bf16[128,8,4096]{2,1,0:T(8,128)(2,1)} broadcast(bf16[8,4096]{1,0:T(8,128)(2,1)S(1)} %dynamic-slice_convert_fusion), dimensions={1,2} | broadcast | bytes 8454144 | tf_op jit(solution)/shard_map/stack | solution.py:62
  73.0 9.7 %all-to-all-start = ((bf16[128,8,4096]{2,1,0:T(8,128)(2,1)}), bf16[128,8,4096]{2,1,0:T(8,128)(2,1)}, u32[]{:S(2)}, u32[]{:S(2)}) async-start(bf16[128,8,4096]{2,1,0:T(8,128)(2,1)} %stack.2), calls=%async_computation | async-start | bytes 16777216 | tf_op jit(solution)/shard_map/all_to_all | solution.py:61
  82.6 0.0 slice-start
  82.6 5.2 %multiply_reduce_fusion.2 = f32[1024]{0:T(1024)S(1)} fusion(bf16[1024,4096]{1,0:T(8,128)(2,1)} %param.4), kind=kLoop, calls=%fused_computation.2 | loop fusion | flops 12581888 | bytes 8392704 | tf_op jit(solution)/shard_map/reduce_sum | solution.py:8
  87.9 0.0 slice-start.1
  87.9 5.2 %multiply_reduce_fusion.1 = f32[1024]{0:T(1024)S(1)} fusion(bf16[1024,4096]{1,0:T(8,128)(2,1)} %all-gather.2.cloned.1.call-done), kind=kLoop, calls=%fused_computation.1 | loop fusion | flops 12581888 | bytes 8392704 | tf_op jit(solution)/shard_map/reduce_sum | solution.py:8
  93.1 0.0 slice-done
  93.1 0.0 slice-done.1
  93.1 12.1 %select_reduce_fusion = f32[1024]{0:T(1024)} fusion(bf16[1024,4096]{1,0:T(8,128)(2,1)} %param.4, bf16[1024,4096]{1,0:T(8,128)(2,1)S(1)} %bitcast.22, f32[1024]{0:T(1024)S(1)} %multiply_reduce_fusion.1, f32[1024]{0:T(1024)S(1)} %multiply_reduce_fusion.2, pred[1024]{0:T(1024)(128)(4,1)S(1)} %fusion.15), kind=kOutput, calls=%fused_computation.7 | convolution fusion | flops 8595176448 | bytes 16790528 | tf_op jit(solution)/shard_map/dot_general | solution.py:12
  105.2 87.5 %all-to-all-done = bf16[128,8,4096]{2,1,0:T(8,128)(2,1)} async-done(((bf16[128,8,4096]{2,1,0:T(8,128)(2,1)}), bf16[128,8,4096]{2,1,0:T(8,128)(2,1)}, u32[]{:S(2)}, u32[]{:S(2)}) %all-to-all-start) | async-done | bytes 8388640 | tf_op jit(solution)/shard_map/all_to_all | solution.py:61
  192.7 5.1 %multiply_reduce_fusion = f32[128,8]{1,0:T(8,128)S(1)} fusion(bf16[128,8,4096]{2,1,0:T(8,128)(2,1)} %all-to-all-done), kind=kLoop, calls=%fused_computation | loop fusion | flops 12581888 | bytes 8392704 | tf_op jit(solution)/shard_map/reduce_sum | solution.py:8
  197.8 0.1 add.62
  197.9 14.6 %fusion.2 = f32[1024]{0:T(1024)} fusion(bf16[1024,4096]{1,0:T(8,128)(2,1)} %param.4, bf16[128,8,4096]{2,1,0:T(8,128)(2,1)} %all-to-all-done, f32[1024]{0:T(1024)S(1)} %add.62, f32[1024]{0:T(1024)S(1)} %multiply_reduce_fusion.2), kind=kOutput, calls=%fused_computation.6 | convolution fusion | flops 8594127872 | bytes 16789504 | tf_op jit(solution)/shard_map/dot_general | solution.py:12
  (7 shorter events, 0.0 us)
Async XLA Ops:
  7.2 56.8 %all-gather.2.cloned.1.call-start = ((), (), s32[]{:S(2)}) async-start(), calls=%async_computation.1 | async-start | bytes 8912896 | tf_op jit(solution)/shard_map/all_gather | solution.py:38
  73.0 119.7 %all-to-all-start = ((bf16[128,8,4096]{2,1,0:T(8,128)(2,1)}), bf16[128,8,4096]{2,1,0:T(8,128)(2,1)}, u32[]{:S(2)}, u32[]{:S(2)}) async-start(bf16[128,8,4096]{2,1,0:T(8,128)(2,1)} %stack.2), calls=%async_computation | async-start | bytes 16777216 | tf_op jit(solution)/shard_map/all_to_all | solution.py:61
  82.6 10.5 %slice-start = ((s8[8388608]{0:T(1024)(128)(4,1)}), s8[4194304]{0:T(1024)(128)(4,1)S(1)}, s32[]{:S(2)}) async-start(s8[8388608]{0:T(1024)(128)(4,1)} %bitcast.21), calls=%async_computation.2 | async-start | bytes 8388608
  87.9 5.2 %slice-start.1 = ((s8[8388608]{0:T(1024)(128)(4,1)}), s8[4194304]{0:T(1024)(128)(4,1)S(1)}, s32[]{:S(2)}) async-start(s8[8388608]{0:T(1024)(128)(4,1)} %bitcast.21), calls=%async_computation.3 | async-start | bytes 8388608
Sparse Core Ops, SparseCore 0:
  9.7 54.2 all-gather.1
